TPU v7x, 256 devices: a whole 4x4x8 slice. The times are simulated.
256 devices in a mesh: seq: 64 (over z, x, core), head: 4 (over y).
Axes of the slice: x: 4, y: 4, z: 8, core: 2. Of those that a mesh axis runs over, the one named last changes fastest.
Arguments:
- ssm_input: float32 [32768, 4096], P('seq', 'head'), may hold values from -50 to 50
- gate_input: bfloat16 [32768, 4096], P('seq', 'head'), may hold values from -6 to 6
- step_raw: float32 [32768, 64], P('seq', 'head'), may hold values from -6 to 65536
- decay_log: float32 [64], P('head')
- state_in: float32 [32768, 4, 128], P('seq', 'head'), may hold values from -0.5 to 0.5
- state_out: float32 [32768, 4, 128], P('seq', 'head'), may hold values from -6 to 6
- skip_gain: float32 [64], P('head'), may hold values from 0.5 to 2
- norm_gain: float32 [4096], P('head'), may hold values from 0.25 to 1.75
- out_weight: bfloat16 [4096, 4096], P('head'), may hold values from -0.09375 to 0.09375
Outputs:
- layer_out: bfloat16 [32768, 4096], P(('seq', 'head'))
All inputs are finite; a program needn't handle non-finite values.
Results may differ from a plain program's by a relative error of at most 0.015.
Values may be sent and summed in bfloat16 or wider, within the bound.
A program may use at most 192 MiB of HBM per device.

v0:
```python
import jax
import jax.numpy as jnp
from jax import lax
from jax.sharding import PartitionSpec as P

HEAD_COUNT = 64
P_SIZE = 64
N = 128
GROUPS = 4
SPAN = 256


def carried_in(value, axis, join, neutral):
    count, mine = (lax.axis_size(axis), lax.axis_index(axis))
    pieces = jax.tree.map(lambda part: lax.all_gather(part, axis), value)
    total = jax.tree.map(
        lambda part, zero: jnp.full_like(part, 0) + jnp.asarray(zero, part.dtype), value, neutral
    )

    def turn(position, total):
        longer = join(total, jax.tree.map(lambda part: part[position], pieces))
        return jax.tree.map(lambda new, old: jnp.where(position < mine, new, old), longer, total)

    return lax.fori_loop(0, count - 1, turn, total)


def link_states(earlier, later):
    return (earlier[0] * later[1][:, None, None] + later[0], earlier[1] * later[1])


def per_device(
    ssm_input,
    gate_input,
    step_raw,
    decay_log,
    state_in,
    state_out,
    skip_gain,
    norm_gain,
    out_weight,
):
    exact = lax.Precision.HIGHEST
    tok_rows = ssm_input.shape[0]
    heads = decay_log.shape[0]
    groups = state_in.shape[1]
    span_count = tok_rows // SPAN
    per_group = heads // groups
    step = jax.nn.softplus(step_raw)
    logdecay = (-step * jnp.exp(decay_log)[None, :]).reshape(span_count, SPAN, heads)
    cumulative = jnp.cumsum(logdecay, axis=1)
    across = jnp.transpose(cumulative, (0, 2, 1))
    causal = jnp.arange(SPAN)[:, None] >= jnp.arange(SPAN)[None, :]
    decays_in = jnp.exp(
        jnp.where(causal[None, None], across[:, :, :, None] - across[:, :, None, :], -jnp.inf)
    )
    inputs = ssm_input.reshape(span_count, SPAN, heads, P_SIZE)
    weighted = inputs * step.reshape(span_count, SPAN, heads)[:, :, :, None]
    in_rows = state_in.reshape(span_count, SPAN, groups, N)
    out_rows = state_out.reshape(span_count, SPAN, groups, N)
    scores = jnp.einsum("cign,cjgn->cgij", out_rows, in_rows, precision=exact)
    mixing = jnp.repeat(scores, per_group, axis=1) * decays_in
    within = jnp.einsum("chij,cjhp->cihp", mixing, weighted, precision=exact)
    in_heads = jnp.repeat(in_rows, per_group, axis=2)
    out_heads = jnp.repeat(out_rows, per_group, axis=2)
    to_end = jnp.exp(cumulative[:, -1:, :] - cumulative)
    span_state = jnp.einsum(
        "cjhp,cjhn->chpn", weighted * to_end[:, :, :, None], in_heads, precision=exact
    )
    span_decay = jnp.exp(cumulative[:, -1, :])
    running = jnp.zeros((heads, P_SIZE, N), jnp.float32)
    lead_decay = jnp.ones((heads,), jnp.float32)
    entering = []
    leading = []
    for position in range(span_count):
        entering.append(running)
        leading.append(lead_decay)
        running = running * span_decay[position][:, None, None] + span_state[position]
        lead_decay = lead_decay * span_decay[position]
    identity = (jnp.zeros((heads, P_SIZE, N), jnp.float32), jnp.ones((heads,), jnp.float32))
    incoming, prior_decay = carried_in((running, lead_decay), "seq", link_states, identity)
    starts = jnp.stack(
        [
            entering[position] + leading[position][:, None, None] * incoming
            for position in range(span_count)
        ]
    )
    carried = (
        jnp.einsum("cihn,chpn->cihp", out_heads, starts, precision=exact)
        * jnp.exp(cumulative)[:, :, :, None]
    )
    ssd = (within + carried).reshape(tok_rows, heads, P_SIZE) + skip_gain[
        None, :, None
    ] * ssm_input.reshape(tok_rows, heads, P_SIZE)
    gated = ssd.reshape(tok_rows, heads * P_SIZE) * jax.nn.silu(gate_input.astype(jnp.float32))
    grouped = gated.reshape(tok_rows, -1, HEAD_COUNT * P_SIZE // GROUPS)
    scaled = grouped * lax.rsqrt(jnp.mean(grouped * grouped, axis=2, keepdims=True) + 1e-05)
    normed = (scaled.reshape(tok_rows, heads * P_SIZE) * norm_gain[None, :]).astype(jnp.bfloat16)
    return lax.psum_scatter(
        jnp.dot(normed, out_weight, preferred_element_type=jnp.float32).astype(jnp.bfloat16),
        "head",
        scatter_dimension=0,
        tiled=True,
    )


def solution(mesh):
    in_specs = (
        P("seq", "head"),
        P("seq", "head"),
        P("seq", "head"),
        P("head"),
        P("seq", "head", None),
        P("seq", "head", None),
        P("head"),
        P("head"),
        P("head", None),
    )
    out_specs = P(("seq", "head"), None)
    return jax.shard_map(
        per_device, mesh=mesh, in_specs=in_specs, out_specs=out_specs, check_vma=False
    )
```

profile of v0, /device:TPU:1, one launch (start us, length us, event | category | flops | bytes accessed | tf_op | source)
XLA Modules:
  0.0 317.1 jit_solution(15877980862023764439)
XLA Ops:
  9.9 1.9 copy.36
  11.8 2.4 reshape.107
  14.2 4.4 %broadcast_multiply_fusion = (f32[2,256,16,64]{1,0,3,2:T(2,128)S(1)}, f32[2,256,16,64]{1,0,3,2:T(2,128)}) fusion(f32[2,256,16]{1,0,2:T(2,128)S(1)} %copy.41, f32[2,256,16,64]{1,0,3,2:T(2,128)} %reshape.107, f32[2,256,16]{1,0,2:T(2,128)S(1)} %mul.134), kind=kLoop, calls=%fused_computation.35 | loop fusion | flops 1048576 | bytes 6356992 | tf_op jit(solution)/shard_map/mul | solution.py:67
  18.6 2.1 fusion.16
  22.7 2.3 copy.45
  25.2 44.2 %all-gather = f32[64,1,16]{2,1,0:T(1,128)S(1)} all-gather(f32[1,1,16]{2,1,0:T(1,128)S(1)} %get-tuple-element.140), channel_id=1, replica_groups=mesh['seq'=64,'head'=4] {'seq'}, dimensions={0}, use_global_device_ids=true | all-gather | bytes 4160 | tf_op jit(solution)/shard_map/all_gather | solution.py:15
  69.9 11.5 %fusion.1 = f32[2,16,64,256]{3,2,1,0:T(8,128)} fusion(f32[2,16,256]{2,1,0:T(8,128)S(1)} %get-tuple-element.137, f32[2,256,256]{2,1,0:T(8,128)S(1)} %fusion.35, pred[256,256]{1,0:T(8,128)(4,1)S(1)} %iota_compare_fusion, f32[2,256,16,64]{1,0,3,2:T(2,128)} %get-tuple-element.131), kind=kOutput, calls=%fused_computation.3 | convolution fusion | flops 1616904192 | bytes 4816896 | tf_op jit(solution)/shard_map/chij,cjhp->cihp/dot_general | solution.py:62
  81.4 88.0 %all-gather.3.cloned.1.call-done = f32[64,16,64,128]{3,2,1,0:T(8,128)} async-done(((f32[1,16,64,128]{3,2,1,0:T(8,128)}), f32[64,16,64,128]{3,2,1,0:T(8,128)}) %all-gather.3.cloned.1.call-update) | async-done | bytes 33554448 | tf_op jit(solution)/shard_map/all_gather | solution.py:15
  169.4 76.5 %while.14 = (s32[]{:T(128)}, f32[16,64,128]{2,1,0:T(8,128)S(1)}, s32[]{:T(128)}, f32[64,16]{1,0:T(8,128)S(1)}, f32[64,16,64,128]{3,2,1,0:T(8,128)}, /*index=5*/s32[]{:T(128)}, s32[]{:T(128)}) while((s32[]{:T(128)}, f32[16,64,128]{2,1,0:T(8,128)S(1)}, s32[]{:T(128)}, f32[64,16]{1,0:T(8,128)S(1)}, f32[64,16,64,128]{3,2,1,0:T(8,128)}, ...), condition=%wide.region_3.4_spmd.clone, body=%wide.region_2.3_spmd.clone.sunk | while | flops 524292 | bytes 1573161 | solution.py:24
  171.9 1.2 fusion.40
  174.3 1.2 fusion.40
  176.7 1.2 fusion.40
  179.2 1.2 fusion.40
  180.4 1.2 fusion.40
  181.6 1.2 fusion.40
  182.8 1.2 fusion.40
  185.2 1.2 fusion.40
  187.7 1.2 fusion.40
  190.1 1.2 fusion.40
  192.5 1.2 fusion.40
  195.0 1.2 fusion.40
  197.4 1.2 fusion.40
  199.8 1.2 fusion.40
  202.2 1.2 fusion.40
  203.4 1.2 fusion.40
  204.7 1.2 fusion.40
  205.9 1.2 fusion.40
  208.3 1.2 fusion.40
  210.7 1.2 fusion.40
  213.2 1.2 fusion.40
  215.6 1.2 fusion.40
  218.0 1.2 fusion.40
  220.4 1.2 fusion.40
  222.9 1.2 fusion.40
  225.3 1.2 fusion.40
  226.5 1.2 fusion.40
  227.7 1.2 fusion.40
  228.9 1.2 fusion.40
  231.4 1.2 fusion.40
  233.8 1.2 fusion.40
  236.2 1.2 fusion.40
  238.7 1.2 fusion.40
  241.1 1.2 fusion.40
  243.5 1.2 fusion.40
  247.1 6.1 %fusion.15 = f32[2,256,16,64]{1,3,2,0:T(8,128)S(1)} fusion(f32[2,16,64,256]{3,2,1,0:T(8,128)} %fusion.1, f32[2,256,128]{2,1,0:T(8,128)S(1)} %bitcast.75, f32[1,16,64,128]{3,2,1,0:T(8,128)S(1)} %fusion.30, f32[1,16,64,128]{3,2,1,0:T(8,128)S(1)} %bitcast.76, f32[2,256,16]{1,2,0:T(8,128)S(1)} %get-tuple-element.132), kind=kOutput, calls=%fused_computation.21 | convolution fusion | flops 806617088 | bytes 5537792 | tf_op jit(solution)/shard_map/cihn,chpn->cihp/dot_general | solution.py:88
  253.2 1.6 copy.43
  257.4 6.7 %convolution_convert_fusion = bf16[512,4096]{1,0:T(8,128)(2,1)} fusion(bf16[1024,4096]{1,0:T(8,128)(2,1)S(1)} %bitcast.84, f32[512,1024]{0,1:T(8,128)S(1)} %get-tuple-element.129, f32[1024]{0:T(1024)S(1)} %copy-done.6, f32[512]{0:T(512)S(1)} %add_rsqrt_fusion), kind=kOutput, calls=%fused_computation.8 | convolution fusion | flops 4298637312 | bytes 14686208 | tf_op jit(solution)/shard_map/dot_general | solution.py:99
  264.1 46.2 %reduce-scatter.2.cloned.1.call-done = bf16[128,4096]{1,0:T(8,128)(2,1)} async-done(((bf16[512,4096]{1,0:T(8,128)(2,1)}), bf16[128,4096]{1,0:T(8,128)(2,1)}) %reduce-scatter.2.cloned.1.call-update) | async-done | bytes 1048592 | tf_op jit(solution)/shard_map/reduce_scatter | solution.py:98
  (139 shorter events, 43.1 us)
Async XLA Ops:
  6.5 62.8 %copy-start = (f32[512,1,128]{2,1,0:T(1,128)S(1)}, f32[512,1,128]{2,1,0:T(1,128)}, u32[]{:S(2)}) copy-start(f32[512,1,128]{2,1,0:T(1,128)} %param.16) | copy-start | bytes 786436
  6.5 162.9 %all-gather.3.cloned.1.call-start = ((), (), s32[]{:S(2)}) async-start(), calls=%async_computation.1 | async-start | bytes 34078720 | tf_op jit(solution)/shard_map/all_gather | solution.py:15
  14.2 4.4 %copy-start.4 = (f32[512,1,128]{2,1,0:T(1,128)S(1)}, f32[512,1,128]{2,1,0:T(1,128)}, u32[]{:S(2)}) copy-start(f32[512,1,128]{2,1,0:T(1,128)} %param.15) | copy-start | bytes 786436
  20.7 1.0 copy-start.2
  21.7 3.3 %copy-start.5 = (f32[16]{0:T(128)S(1)}, f32[16]{0:T(128)}, u32[]{:S(2)}) copy-start(f32[16]{0:T(128)} %param.17) | copy-start | bytes 196
  22.7 287.6 %reduce-scatter.2.cloned.1.call-start = ((), (), s32[]{:S(2)}) async-start(), calls=%async_computation.2 | async-start | bytes 5242880 | tf_op jit(solution)/shard_map/reduce_scatter | solution.py:98
  247.1 9.9 %slice-start = ((s8[8388608]{0:T(1024)(128)(4,1)}), s8[4194304]{0:T(1024)(128)(4,1)S(1)}, s32[]{:S(2)}) async-start(s8[8388608]{0:T(1024)(128)(4,1)} %bitcast.83), calls=%async_computation.3 | async-start | bytes 8388608
  254.9 1.2 copy-start.3
  254.9 2.5 slice-start.1
  256.1 1.3 copy-start.6
  264.0 46.2 %copy-start.1 = (f32[512,1,128]{2,1,0:T(1,128)S(1)}, f32[512,1,128]{2,1,0:T(1,128)}, u32[]{:S(2)}) copy-start(f32[512,1,128]{2,1,0:T(1,128)} %param.16) | copy-start | bytes 786436
Sparse Core Ops, SparseCore 0:
  22.8 146.6 all-gather.2
  264.2 46.0 reduce-scatter.1
where the time goes:
time: 320 us; the launch traced here: 317 us
  waiting for transfers between devices  134 us (42%)
  other arithmetic  83.4 us (26%)
  blocking collectives  44.2 us (14%)
  matrix products  27 us (8%)
  between operations  13.6 us (4%)
  local copies, waits for them, and re-layouts  12.7 us (4%)
    all_gather x1, waiting for transfers between devices, carried_in(): pieces = jax.tree.map(lambda part: lax.all_gather(part, axis), value)  88 us
    select_n x63, other arithmetic, turn(): jnp.where(position < mine, new, old)  73.9 us
    reduce_scatter x1, waiting for transfers between devices, per_device(): lax.psum_scatter(jnp.dot(normed, out_weight, preferred_element_type=jnp.f...  46.2 us
    all_gather x1, blocking collectives, carried_in(): pieces = jax.tree.map(lambda part: lax.all_gather(part, axis), value)  44.2 us
    dot_general x1, matrix products, per_device(): within = jnp.einsum('chij,cjhp->cihp', mixing, weighted, precision=exact)  11.5 us
    unnamed x21, local copies, waits for them, and re-layouts  6.85 us
    dot_general x1, matrix products, per_device(): jnp.dot(normed, out_weight, preferred_element_type=jnp.float32)  6.66 us
  transfers between devices with their start and end apart: 2, of which 2 were waited for; matrix products, arithmetic and copies ran while one was open for 5% of the time, Pallas kernels for 0%

commit v1 on v0

v1 whole, which is shorter than its diff:
```python
import functools

import jax
import jax.numpy as jnp
from jax import lax
from jax.experimental import pallas as pl
from jax.experimental.pallas import tpu as pltpu
from jax.sharding import PartitionSpec as P

F32, BF16 = jnp.float32, jnp.bfloat16
P_SIZE = 64
N = 128
BLOCK = 128
ROW = 8
PIECE = 512
LANES = 128
EXACT = lax.Precision.HIGHEST
MESH = pl.DeviceIdType.MESH


def dot(a, b):
    return jnp.dot(a, b, preferred_element_type=F32)


def exact_dot(a, b):
    return jnp.dot(a, b, preferred_element_type=F32, precision=EXACT)


def stack_rows(rows, count):
    where_row = lax.broadcasted_iota(jnp.int32, (count, rows[0].shape[1]), 0)
    out = jnp.zeros((count, rows[0].shape[1]), F32)
    for k, row in enumerate(rows):
        out = jnp.where(where_row == k, jnp.broadcast_to(row, out.shape), out)
    return out


def kernel(
    row_n, z_n, y_n,
    x_hbm, g_hbm, sr_hbm, dl_ref, b_hbm, c_hbm, sk_ref, ng_ref, w_hbm,
    o_hbm,
    xv, gv, srv, bv, cv, wv,
    spread, step_s, cum_s, cum_t, ecum_s, b_t, c_b,
    sent, lead, sbuf, rbuf, tbuf, ubuf, zs, zr, lt, lr, zt, zl, pre,
    yw, sg, nb, own,
    so, s_right, s_left, ro_left, ro_right, rf_left, rf_right, ob,
    in_sem, row_s, row_r, log_s, log_r, z_s, z_r, zlog_s, zlog_r, back_s, back_r, sum_s, sum_r, out_sem,
):
    tokens, width = xv.shape
    heads = srv.shape[1]
    blocks = tokens // BLOCK
    pieces = wv.shape[1] // PIECE
    half = pieces // 2
    me = lax.axis_index("seq")
    y = lax.axis_index("head")
    z, r = lax.div(me, row_n), lax.rem(me, row_n)
    right, left, opp = lax.rem(y + 1, y_n), lax.rem(y + y_n - 1, y_n), lax.rem(y + 2, y_n)

    def row_peer(j):
        return lax.rem(r + j, row_n)

    def z_peer(j):
        return lax.rem(z + j, z_n)

    barrier = pltpu.get_barrier_semaphore()
    for j in range(1, row_n):
        pl.semaphore_signal(barrier, inc=1, device_id=(z * row_n + row_peer(j), y), device_id_type=MESH)
    for j in range(1, z_n):
        pl.semaphore_signal(barrier, inc=1, device_id=(z_peer(j) * row_n + r, y), device_id_type=MESH)
    for side in (right, left):
        pl.semaphore_signal(barrier, inc=1, device_id=(me, side), device_id_type=MESH)

    loads = [
        pltpu.make_async_copy(src, dst, in_sem.at[k])
        for k, (src, dst) in enumerate(
            ((sr_hbm, srv), (b_hbm, bv), (x_hbm, xv), (c_hbm, cv), (g_hbm, gv), (w_hbm, wv))
        )
    ]
    for load in loads:
        load.start()

    head_of = lax.broadcasted_iota(jnp.int32, (heads, width), 1) // P_SIZE
    spread[...] = jnp.where(head_of == lax.broadcasted_iota(jnp.int32, (heads, width), 0), 1.0, 0.0).astype(BF16)

    def spread_rows(rows):
        return exact_dot(rows, spread[...].astype(F32))

    loads[0].wait()
    raw = srv[...]
    step = jnp.maximum(raw, 0.0) + jnp.log1p(jnp.exp(-jnp.abs(raw)))
    step_s[...] = step.astype(BF16)
    logdecay = -step * jnp.exp(dl_ref[...])
    row_i = lax.broadcasted_iota(jnp.int32, (BLOCK, BLOCK), 0)
    col_i = lax.broadcasted_iota(jnp.int32, (BLOCK, BLOCK), 1)
    lower = jnp.where(row_i >= col_i, 1.0, 0.0)
    totals, leads, ends = [], [], []
    so_far = jnp.zeros((1, heads), F32)
    for c in range(blocks):
        rows = slice(c * BLOCK, (c + 1) * BLOCK)
        cum = exact_dot(lower, logdecay[rows])
        cum_s[rows] = cum
        cum_t[c] = jnp.transpose(cum)
        ecum_s[rows] = jnp.exp(cum).astype(BF16)
        total = cum[BLOCK - 1 : BLOCK]
        ends.append((step[rows] * jnp.exp(total - cum)).astype(BF16))
        totals.append(total)
        leads.append(so_far)
        so_far = so_far + total
    lt[...] = jnp.zeros(lt.shape, F32)
    lt[:, 0:heads] = jnp.broadcast_to(so_far, (8, heads))
    factors = spread_rows(jnp.exp(stack_rows(totals + leads, 8)))
    for c in range(blocks):
        lead[c] = jnp.broadcast_to(factors[blocks + c : blocks + c + 1], (8, width))

    loads[1].wait()
    for c in range(blocks):
        b_t[c] = jnp.transpose(bv[c * BLOCK : (c + 1) * BLOCK, :]).astype(BF16)
    loads[2].wait()
    tile = 256
    for t in range(width // tile):
        lanes = slice(t * tile, (t + 1) * tile)
        state = jnp.zeros((N, tile), F32)
        for c in range(blocks):
            rows = slice(c * BLOCK, (c + 1) * BLOCK)
            sent[c, :, lanes] = state
            ended = (xv[rows, lanes] * dot(ends[c], spread[:, lanes])).astype(BF16)
            state = state * factors[c : c + 1, lanes] + dot(b_t[c], ended)
        sbuf[:, :, lanes] = state.astype(BF16).reshape(row_n, N // row_n, tile)

    pl.semaphore_wait(barrier, row_n - 1 + z_n - 1 + 2)

    def row_copies(j):
        k = row_peer(j)
        where = (z * row_n + k, y)
        return (
            pltpu.make_async_remote_copy(lt, lr.at[r], log_s.at[j], log_r.at[j], device_id=where, device_id_type=MESH),
            pltpu.make_async_remote_copy(
                sbuf.at[k], rbuf.at[r], row_s.at[j], row_r.at[j], device_id=where, device_id_type=MESH
            ),
        )

    for j in range(1, row_n):
        for copy in row_copies(j):
            copy.start()
    lr[r] = lt[...]
    rbuf[r] = sbuf[r]

    first_half = lax.broadcasted_iota(jnp.int32, (BLOCK, LANES), 1) < P_SIZE
    loads[3].wait()
    c_b[...] = cv[...].astype(BF16)
    loads[4].wait()
    skip = spread_rows(jnp.broadcast_to(sk_ref[...], (8, heads)))

    def within(c, carry):
        rows = pl.ds(pl.multiple_of(c * BLOCK, BLOCK), BLOCK)
        scores = jnp.where(row_i >= col_i, dot(c_b[rows, :], b_t[c]), 0.0)
        cum = cum_s[rows, :]
        across = cum_t[c]
        steps = step_s[rows, :]
        for pair in range(width // LANES):
            lanes = slice(pair * LANES, (pair + 1) * LANES)
            mixes = []
            for h in (2 * pair, 2 * pair + 1):
                gap = jnp.minimum(cum[:, h : h + 1] - across[h : h + 1, :], 0.0)
                mixes.append((scores * jnp.exp(gap)).astype(BF16))
            x = xv[rows, lanes]
            weighted = x * dot(steps, spread[:, lanes])
            both = jnp.concatenate(
                [jnp.where(first_half, weighted, 0.0), jnp.where(first_half, 0.0, weighted)], axis=0
            ).astype(BF16)
            yw[rows, lanes] = dot(jnp.concatenate(mixes, axis=1), both) + skip[0:1, lanes] * x
            gate = gv[rows, lanes].astype(F32)
            sg[rows, lanes] = gate / (1.0 + jnp.exp(-gate))
        return carry

    lax.fori_loop(0, blocks // 2, within, 0)

    for j in range(1, row_n):
        for copy in row_copies(j):
            copy.wait_recv()
    logs = [lr[k][0:1, 0:heads] for k in range(row_n)]
    ahead, running = [], jnp.zeros((1, heads), F32)
    for log in logs:
        ahead.append(running)
        running = running + log
    decay_row = spread_rows(jnp.exp(stack_rows(logs, 8)))
    ahead_row = spread_rows(jnp.exp(stack_rows(ahead, 8)))
    state = jnp.zeros((N // row_n, width), F32)
    for k in range(row_n):
        pre[k] = state
        state = state * decay_row[k : k + 1] + rbuf[k].astype(F32)
    zs[...] = state.astype(BF16)
    zt[...] = jnp.zeros(zt.shape, F32)
    zt[:, 0:heads] = jnp.broadcast_to(running, (8, heads))

    def z_copies(j):
        where = (z_peer(j) * row_n + r, y)
        return (
            pltpu.make_async_remote_copy(zt, zl.at[z], zlog_s.at[j], zlog_r.at[j], device_id=where, device_id_type=MESH),
            pltpu.make_async_remote_copy(zs, zr.at[z], z_s.at[j], z_r.at[j], device_id=where, device_id_type=MESH),
        )

    for j in range(1, z_n):
        for copy in z_copies(j):
            copy.start()
    zl[z] = zt[...]
    zr[z] = zs[...]

    lax.fori_loop(blocks // 2, blocks, within, 0)

    for j in range(1, z_n):
        for copy in z_copies(j):
            copy.wait_recv()
    decay_z = spread_rows(jnp.exp(stack_rows([zl[k][0:1, 0:heads] for k in range(z_n)], 8)))
    incoming = jnp.zeros((N // row_n, width), F32)
    for k in range(z_n - 1):
        incoming = jnp.where(k < z, incoming * decay_z[k : k + 1] + zr[k].astype(F32), incoming)
    for k in range(row_n):
        tbuf[k] = (pre[k] + incoming * ahead_row[k : k + 1]).astype(BF16)

    def back_copy(j):
        k = row_peer(j)
        return pltpu.make_async_remote_copy(
            tbuf.at[k], ubuf.at[r], back_s.at[j], back_r.at[j], device_id=(z * row_n + k, y), device_id_type=MESH
        )

    for j in range(1, row_n):
        back_copy(j).start()
    ubuf[r] = tbuf[r]
    loads[5].wait()
    for j in range(1, row_n):
        back_copy(j).wait_recv()

    def norm(d):
        rows = pl.ds(pl.multiple_of(d * BLOCK, BLOCK), BLOCK)
        led = lead[d]
        squares = jnp.zeros((BLOCK, 1), F32)
        c_rows = c_b[rows, :]
        decays = ecum_s[rows, :]
        for t in range(width // tile):
            lanes = slice(t * tile, (t + 1) * tile)
            came = ubuf[:, :, lanes].reshape(N, tile).astype(F32)
            entering = (sent[d, :, lanes] + led[0:1, lanes] * came).astype(BF16)
            ssd = yw[rows, lanes] + dot(c_rows, entering) * dot(decays, spread[:, lanes])
            gated = ssd * sg[rows, lanes]
            squares = squares + jnp.sum(gated * gated, axis=1, keepdims=True)
            sg[rows, lanes] = gated
        scale = lax.rsqrt(squares * (1.0 / width) + 1e-05)
        for t in range(width // tile):
            lanes = slice(t * tile, (t + 1) * tile)
            nb[rows, lanes] = (sg[rows, lanes] * scale * ng_ref[:, lanes]).astype(BF16)

    def product(d, p):
        rows = pl.ds(pl.multiple_of(d * BLOCK, BLOCK), BLOCK)
        return dot(nb[rows, :], wv[:, pl.ds(pl.multiple_of(p * PIECE, PIECE), PIECE)])

    def far_right(i):
        return pltpu.make_async_remote_copy(
            so.at[i], ro_left.at[i], sum_s.at[i], sum_r.at[i], device_id=(me, right), device_id_type=MESH
        )

    def far_left(i):
        return pltpu.make_async_remote_copy(
            so.at[half + i], ro_right.at[i], sum_s.at[half + i], sum_r.at[half + i],
            device_id=(me, left), device_id_type=MESH,
        )

    def to_right(p):
        return pltpu.make_async_remote_copy(
            s_right.at[p], rf_left.at[p], sum_s.at[pieces + p], sum_r.at[pieces + p],
            device_id=(me, right), device_id_type=MESH,
        )

    def to_left(p):
        return pltpu.make_async_remote_copy(
            s_left.at[p], rf_right.at[p], sum_s.at[2 * pieces + p], sum_r.at[2 * pieces + p],
            device_id=(me, left), device_id_type=MESH,
        )

    def out_copy(p):
        return pltpu.make_async_copy(
            ob.at[p], o_hbm.at[:, pl.ds(pl.multiple_of(p * PIECE, PIECE), PIECE)], out_sem.at[p]
        )

    norm(opp)

    def far_step(i, carry):
        so[i] = product(opp, i).astype(BF16)
        far_right(i).start()
        so[half + i] = product(opp, half + i).astype(BF16)
        far_left(i).start()
        return carry

    lax.fori_loop(0, half, far_step, 0)
    norm(right)
    norm(left)

    def near_step(i, carry):
        s_right[half + i] = product(right, half + i).astype(BF16)
        to_right(half + i).start()
        s_left[i] = product(left, i).astype(BF16)
        to_left(i).start()
        return carry

    lax.fori_loop(0, half, near_step, 0)
    norm(y)

    def own_step(p, carry):
        own[p] = product(y, p)
        return carry

    lax.fori_loop(0, pieces, own_step, 0)

    def sum_step(i, carry):
        ahead_right = product(right, i)
        ahead_left = product(left, half + i)
        far_right(i).wait_recv()
        s_right[i] = (ahead_right + ro_left[i].astype(F32)).astype(BF16)
        to_right(i).start()
        far_left(i).wait_recv()
        s_left[half + i] = (ahead_left + ro_right[i].astype(F32)).astype(BF16)
        to_left(half + i).start()
        return carry

    lax.fori_loop(0, half, sum_step, 0)

    def last_step(i, carry):
        for p in (i, half + i):
            to_right(p).wait_recv()
            to_left(p).wait_recv()
            ob[p] = (own[p] + rf_left[p].astype(F32) + rf_right[p].astype(F32)).astype(BF16)
            out_copy(p).start()
        return carry

    lax.fori_loop(0, half, last_step, 0)

    for j in range(1, row_n):
        for copy in row_copies(j):
            copy.wait_send()
        back_copy(j).wait_send()
    for j in range(1, z_n):
        for copy in z_copies(j):
            copy.wait_send()

    def drain(i, carry):
        far_right(i).wait_send()
        far_left(i).wait_send()
        for p in (i, half + i):
            to_right(p).wait_send()
            to_left(p).wait_send()
            out_copy(p).wait()
        return carry

    lax.fori_loop(0, half, drain, 0)


def solution(mesh):
    y_n = mesh.shape["head"]
    row_n = ROW
    z_n = mesh.shape["seq"] // row_n

    def per_device(x, g, sr, dl, b, c, sk, ng, w):
        tokens, width = x.shape
        heads = dl.shape[0]
        dout = w.shape[1]
        blocks = tokens // BLOCK
        pieces = dout // PIECE
        slab = N // row_n
        any_spec = pl.BlockSpec(memory_space=pl.ANY)
        vmem_spec = pl.BlockSpec(memory_space=pltpu.VMEM)
        dma = pltpu.SemaphoreType.DMA
        vmem = pltpu.VMEM
        half = (pieces // 2, BLOCK, PIECE)
        full = (pieces, BLOCK, PIECE)
        return pl.pallas_call(
            functools.partial(kernel, row_n, z_n, y_n),
            out_shape=jax.ShapeDtypeStruct((tokens // y_n, dout), BF16),
            in_specs=[any_spec] * 3 + [vmem_spec] + [any_spec] * 2 + [vmem_spec] * 2 + [any_spec],
            out_specs=any_spec,
            scratch_shapes=[
                vmem((tokens, width), F32), vmem((tokens, width), BF16), vmem((tokens, heads), F32),
                vmem((tokens, N), F32), vmem((tokens, N), F32), vmem(w.shape, BF16),
                vmem((heads, width), BF16), vmem((tokens, heads), BF16), vmem((tokens, heads), F32),
                vmem((blocks, heads, BLOCK), F32), vmem((tokens, heads), BF16),
                vmem((blocks, N, BLOCK), BF16), vmem((tokens, N), BF16),
                vmem((blocks, N, width), F32), vmem((blocks, 8, width), F32),
                vmem((row_n, slab, width), BF16), vmem((row_n, slab, width), BF16),
                vmem((row_n, slab, width), BF16), vmem((row_n, slab, width), BF16),
                vmem((slab, width), BF16), vmem((z_n, slab, width), BF16),
                vmem((8, LANES), F32), vmem((row_n, 8, LANES), F32),
                vmem((8, LANES), F32), vmem((z_n, 8, LANES), F32),
                vmem((row_n, slab, width), F32),
                vmem((tokens, width), F32), vmem((tokens, width), F32), vmem((tokens, width), BF16),
                vmem(full, F32),
                vmem(full, BF16), vmem(full, BF16), vmem(full, BF16),
                vmem(half, BF16), vmem(half, BF16), vmem(full, BF16), vmem(full, BF16), vmem(full, BF16),
                dma((6,)), dma((row_n,)), dma((row_n,)), dma((row_n,)), dma((row_n,)),
                dma((z_n,)), dma((z_n,)), dma((z_n,)), dma((z_n,)), dma((row_n,)), dma((row_n,)),
                dma((3 * pieces,)), dma((3 * pieces,)), dma((pieces,)),
            ],
            compiler_params=pltpu.CompilerParams(
                collective_id=0, has_side_effects=True, vmem_limit_bytes=60 * 1024 * 1024
            ),
        )(
            x, g, sr, dl.reshape(1, heads), b.reshape(tokens, N), c.reshape(tokens, N),
            sk.reshape(1, heads), ng.reshape(1, width), w,
        )

    in_specs = (
        P("seq", "head"), P("seq", "head"), P("seq", "head"), P("head"), P("seq", "head", None),
        P("seq", "head", None), P("head"), P("head"), P("head", None),
    )
    return jax.shard_map(
        per_device, mesh=mesh, in_specs=in_specs, out_specs=P(("seq", "head"), None), check_vma=False
    )
```

time: 320 us -> 73 us (0.23)
  waiting for transfers between devices: 134 us -> 0 us
  other arithmetic: 83.4 us -> 0 us
  Pallas kernels: 0 us -> 68.9 us
  blocking collectives: 44.2 us -> 0 us
  matrix products: 27 us -> 0 us
  between operations: 13.6 us -> 0.01 us
  local copies, waits for them, and re-layouts: 12.7 us -> 3.88 us
    all_gather x1 -> x0, waiting for transfers between devices: 88 us -> none  [carried_in(): pieces = jax.tree.map(lambda part: lax.all_gather(part, axis), value)]
    select_n x64 -> x0, other arithmetic: 74.7 us -> none  [the longest x63 73.9 us: turn(): jnp.where(position < mine, new, old)]
    pallas_call x0 -> x1, Pallas kernels: none -> 68.9 us  [per_device(): pl.pallas_call(functools.partial(kernel, row_n, z_n, y_n), out_shape=jax....]
    reduce_scatter x1 -> x0, waiting for transfers between devices: 46.2 us -> none  [per_device(): lax.psum_scatter(jnp.dot(normed, out_weight, preferred_element_type=jnp.f...]
    all_gather x1 -> x0, blocking collectives: 44.2 us -> none  [carried_in(): pieces = jax.tree.map(lambda part: lax.all_gather(part, axis), value)]
    dot_general x5 -> x0, matrix products: 27 us -> none  [the longest x1 11.5 us: per_device(): within = jnp.einsum('chij,cjhp->cihp', mixing, weighted, precision=exact)]
    mul x2 -> x0, other arithmetic: 4.38 us -> none  [the longest x1 4.37 us: per_device(): weighted * to_end[:, :, :, None]]
    unnamed x21 -> x2, local copies, waits for them, and re-layouts: 6.85 us -> 3.88 us
  transfers between devices with their start and end apart: 2 -> 0, of which waited for: 2 -> 0; matrix products, arithmetic and copies ran while one was open for 5% -> 0% of each run, Pallas kernels for 0% -> 0%
where the time goes in v1:
time: 73 us; the launch traced here: 72.8 us
  Pallas kernels  68.9 us (94%)
  local copies, waits for them, and re-layouts  3.88 us (5%)
    pallas_call x1, Pallas kernels, per_device(): pl.pallas_call(functools.partial(kernel, row_n, z_n, y_n), out_shape=jax....  68.9 us
    unnamed x2, local copies, waits for them, and re-layouts  3.88 us

profile of v1, /device:TPU:1, one launch (start us, length us, event | category | flops | bytes accessed | tf_op | source)
XLA Modules:
  0.0 72.8 jit_solution(3459581753683468196)
XLA Ops:
  0.0 1.6 %copy.10.sr_hbm = f32[512,16]{1,0:T(8,128)} copy(f32[512,16]{0,1:T(8,128)} %param.11) | data formatting | bytes 65536 | tf_op args[2]
  1.6 68.9 %shard_map.91 = bf16[128,4096]{1,0:T(8,128)(2,1)} custom-call(f32[512,1024]{1,0:T(8,128)} %x_hbm.1, bf16[512,1024]{1,0:T(8,128)(2,1)} %g_hbm.1, f32[512,16]{1,0:T(8,128)} %copy.10.sr_hbm, f32[1,16]{1,0:T(1,128)} %bitcast.8, f32[512,128]{1,0:T(8,128)} %bitcast.5, f32[512,128]{1,0:T(8,128)} %bitcast.6, f32[1,16]{1,0:T(1,128)} %bitcast.9, f32[1,1024]{1,0:T(1,128)} %bitcast.7, ...), custom_call_target="tpu_custom_call" | custom-call | tf_op jit(solution)/shard_map/pallas_call | solution.py:374
  70.5 2.3 %copy.12 = bf16[128,4096]{1,0:T(8,128)(2,1)} copy(bf16[128,4096]{1,0:T(8,128)(2,1)} %shard_map.91) | data formatting | bytes 2097152

commit v2 on v1

v2 whole, which is shorter than its diff:
```python
import functools

import jax
import jax.numpy as jnp
from jax import lax
from jax.experimental import pallas as pl
from jax.experimental.pallas import tpu as pltpu
from jax.sharding import PartitionSpec as P

F32, BF16 = jnp.float32, jnp.bfloat16
P_SIZE = 64
N = 128
BLOCK = 128
CORES = 2
X = 4
ROW = CORES * X
GROUP = 4
PIECE = 512
LANES = 128
EXACT = lax.Precision.HIGHEST
MESH = pl.DeviceIdType.MESH


def dot(a, b):
    return jnp.dot(a, b, preferred_element_type=F32)


def exact_dot(a, b):
    return jnp.dot(a, b, preferred_element_type=F32, precision=EXACT)


def stack_rows(rows, count):
    where_row = lax.broadcasted_iota(jnp.int32, (count, rows[0].shape[1]), 0)
    out = jnp.zeros((count, rows[0].shape[1]), F32)
    for k, row in enumerate(rows):
        out = jnp.where(where_row == k, jnp.broadcast_to(row, out.shape), out)
    return out


def kernel(
    z_n, y_n,
    x_hbm, g_hbm, sr_hbm, dl_ref, b_hbm, c_hbm, sk_ref, ng_ref, w_hbm,
    ob,
    xv, gv, srv, bv, cv, wv,
    spread, spread_col, cum_t, cols_s, cols_b, b_t, c_b,
    sent, lead, sbuf, cbuf, xs, xr, bs, br, cs, ubuf, zs, zr, ps, pr,
    lt, cl, xt, xl, zt, zl, pre, zin,
    yw, sg, nb, own,
    so, s_right, s_left, ro_left, ro_right, rf_left, rf_right,
    in_sem, core_s, core_r, x_s, x_r, xlog_s, xlog_r, z_s, z_r, zlog_s, zlog_r, p_s, p_r, back_s, back_r, sum_s, sum_r,
):
    tokens, width = xv.shape
    heads = srv.shape[0]
    blocks = tokens // BLOCK
    pieces = wv.shape[1] // PIECE
    half = pieces // 2
    slab = N // ROW
    me = lax.axis_index("seq")
    y = lax.axis_index("head")
    z, r = lax.div(me, ROW), lax.rem(me, ROW)
    x_at, core = lax.div(r, CORES), lax.rem(r, CORES)
    z_in = lax.rem(z, GROUP)
    right, left, opp = lax.rem(y + 1, y_n), lax.rem(y + y_n - 1, y_n), lax.rem(y + 2, y_n)
    sibling = (me + 1 - 2 * core, y)
    gate_z = GROUP - 1

    def x_peer(j):
        return lax.rem(x_at + j, X)

    def at_x(k):
        return (z * ROW + k * CORES + core, y)

    def at_z(k):
        return (k * ROW + r, y)

    barrier = pltpu.get_barrier_semaphore()

    def greet(where):
        pl.semaphore_signal(barrier, inc=1, device_id=where, device_id_type=MESH)

    greet(sibling)
    for j in range(1, X):
        greet(at_x(x_peer(j)))
    greet((me, right))
    greet((me, left))
    for j in range(1, GROUP):
        pl.when(z_in >= j)(functools.partial(greet, at_z(z - j)))
    pl.when(z >= GROUP)(functools.partial(greet, at_z(gate_z)))

    loads = [
        pltpu.make_async_copy(src, dst, in_sem.at[k])
        for k, (src, dst) in enumerate(
            ((sr_hbm, srv), (b_hbm, bv), (x_hbm, xv), (c_hbm, cv), (g_hbm, gv), (w_hbm, wv))
        )
    ]
    for load in loads[:3]:
        load.start()

    head_of = lax.broadcasted_iota(jnp.int32, (heads, width), 1) // P_SIZE
    spread[...] = jnp.where(head_of == lax.broadcasted_iota(jnp.int32, (heads, width), 0), 1.0, 0.0).astype(BF16)
    spread_col[...] = jnp.zeros(spread_col.shape, BF16)
    for k in range(1, 4):
        spread_col[k, k * heads : (k + 1) * heads, :] = spread[...]

    def spread_rows(rows):
        high = rows.astype(BF16)
        return dot(high, spread[...]) + dot((rows - high.astype(F32)).astype(BF16), spread[...])

    def tile_of(row):
        return jnp.concatenate([row, jnp.zeros((1, LANES - heads), F32)], axis=1)

    loads[0].wait()
    rate = jnp.transpose(jnp.broadcast_to(jnp.exp(dl_ref[...]), (BLOCK, heads)))
    row_i = lax.broadcasted_iota(jnp.int32, (BLOCK, BLOCK), 0)
    col_i = lax.broadcasted_iota(jnp.int32, (BLOCK, BLOCK), 1)
    upper = jnp.where(row_i <= col_i, 1.0, 0.0)
    totals, leads = [], []
    so_far = jnp.zeros((1, heads), F32)
    for c in range(blocks):
        raw = srv[:, c * BLOCK : (c + 1) * BLOCK]
        step = jnp.maximum(raw, 0.0) + jnp.log1p(jnp.exp(-jnp.abs(raw)))
        cum = exact_dot(-step * rate, upper)
        cum_t[c] = cum
        to_end = step * jnp.exp(cum[:, BLOCK - 1 : BLOCK] - cum)
        cols = jnp.transpose(jnp.concatenate([cum, to_end, jnp.exp(cum), step], axis=0))
        cols_s[c] = cols
        cols_b[c] = cols.astype(BF16)
        total = cols[BLOCK - 1 : BLOCK, 0:heads]
        totals.append(total)
        leads.append(so_far)
        so_far = so_far + total
    lt[...] = jnp.zeros(lt.shape, F32)
    lt[:, 0:heads] = jnp.broadcast_to(so_far, (8, heads))
    factors = spread_rows(jnp.exp(stack_rows(totals + leads, 8)))
    for c in range(blocks):
        lead[c] = jnp.broadcast_to(factors[blocks + c : blocks + c + 1], (8, width))

    loads[1].wait()
    for c in range(blocks):
        b_t[c] = jnp.transpose(bv[c * BLOCK : (c + 1) * BLOCK, :]).astype(BF16)
    loads[2].wait()
    for load in loads[3:]:
        load.start()
    tile = 256
    for t in range(width // tile):
        lanes = slice(t * tile, (t + 1) * tile)
        state = jnp.zeros((N, tile), F32)
        for c in range(blocks):
            rows = slice(c * BLOCK, (c + 1) * BLOCK)
            sent[c, :, lanes] = state
            ended = (xv[rows, lanes] * dot(cols_b[c], spread_col[1, :, lanes])).astype(BF16)
            state = state * factors[c : c + 1, lanes] + dot(b_t[c], ended)
        sbuf[:, :, :, lanes] = state.astype(BF16).reshape(CORES, X, slab, tile)

    pl.semaphore_wait(barrier, X + 2 + (GROUP - 1 - z_in) + jnp.where(z == gate_z, z_n - GROUP, 0))

    core_log = pltpu.make_async_remote_copy(
        lt, cl.at[core], core_s.at[0], core_r.at[0], device_id=sibling, device_id_type=MESH
    )
    core_state = pltpu.make_async_remote_copy(
        sbuf.at[1 - core], cbuf.at[core], core_s.at[1], core_r.at[1], device_id=sibling, device_id_type=MESH
    )
    core_log.start()
    core_state.start()
    cl[core] = lt[...]
    cbuf[core] = sbuf[core]
    core_log.wait_recv()
    log_first, log_second = cl[0][0:1, 0:heads], cl[1][0:1, 0:heads]
    decay_core = spread_rows(jnp.exp(stack_rows([log_first, log_second], 8)))
    xt[...] = cl[0] + cl[1]
    core_state.wait_recv()
    for k in range(X):
        xs[k] = (cbuf[0, k].astype(F32) * decay_core[1:2] + cbuf[1, k].astype(F32)).astype(BF16)

    def x_copies(j):
        k = x_peer(j)
        return (
            pltpu.make_async_remote_copy(
                xt, xl.at[x_at], xlog_s.at[j], xlog_r.at[j], device_id=at_x(k), device_id_type=MESH
            ),
            pltpu.make_async_remote_copy(
                xs.at[k], xr.at[x_at], x_s.at[j], x_r.at[j], device_id=at_x(k), device_id_type=MESH
            ),
        )

    for j in (2, 1, 3):
        for copy in x_copies(j):
            copy.start()
    xl[x_at] = xt[...]
    xr[x_at] = xs[x_at]

    first_half = lax.broadcasted_iota(jnp.int32, (BLOCK, LANES), 1) < P_SIZE
    loads[3].wait()
    c_b[...] = cv[...].astype(BF16)
    loads[4].wait()
    skip = spread_rows(jnp.broadcast_to(sk_ref[...], (8, heads)))

    def within(c, carry):
        rows = pl.ds(pl.multiple_of(c * BLOCK, BLOCK), BLOCK)
        scores = jnp.where(row_i >= col_i, dot(c_b[rows, :], b_t[c]), 0.0)
        cum = cols_s[c]
        across = cum_t[c]
        cols = cols_b[c]
        for pair in range(width // LANES):
            lanes = slice(pair * LANES, (pair + 1) * LANES)
            mixes = []
            for h in (2 * pair, 2 * pair + 1):
                gap = jnp.minimum(cum[:, h : h + 1] - across[h : h + 1, :], 0.0)
                mixes.append((scores * jnp.exp(gap)).astype(BF16))
            x = xv[rows, lanes]
            weighted = x * dot(cols, spread_col[3, :, lanes])
            both = jnp.concatenate(
                [jnp.where(first_half, weighted, 0.0), jnp.where(first_half, 0.0, weighted)], axis=0
            ).astype(BF16)
            yw[rows, lanes] = dot(jnp.concatenate(mixes, axis=1), both) + skip[0:1, lanes] * x
            gate = gv[rows, lanes].astype(F32)
            sg[rows, lanes] = gate / (1.0 + jnp.exp(-gate))
        return carry

    lax.fori_loop(0, blocks - 1, within, 0)

    for j in range(1, X):
        for copy in x_copies(j):
            copy.wait_recv()
    logs = [xl[k][0:1, 0:heads] for k in range(X)]
    ahead, running = [], jnp.zeros((1, heads), F32)
    for log in logs:
        ahead.append(running)
        running = running + log
    decay_row = spread_rows(jnp.exp(stack_rows(logs + ahead, 8)))
    state = jnp.zeros((slab, width), F32)
    for k in range(X):
        pre[k] = state
        state = state * decay_row[k : k + 1] + xr[k].astype(F32)
    zs[...] = state.astype(BF16)
    zt[...] = jnp.zeros(zt.shape, F32)
    zt[:, 0:heads] = jnp.broadcast_to(running, (8, heads))

    def z_copies(j, to):
        return (
            pltpu.make_async_remote_copy(
                zt, zl.at[z_in], zlog_s.at[j], zlog_r.at[j], device_id=at_z(to), device_id_type=MESH
            ),
            pltpu.make_async_remote_copy(
                zs, zr.at[z_in], z_s.at[j], z_r.at[j], device_id=at_z(to), device_id_type=MESH
            ),
        )

    def z_send(j):
        for copy in z_copies(j, z + j):
            copy.start()

    def z_take(j):
        for copy in z_copies(j, z):
            copy.wait_recv()

    def z_sent(j):
        for copy in z_copies(j, z + j):
            copy.wait_send()

    for j in range(1, GROUP):
        pl.when(z_in + j < GROUP)(functools.partial(z_send, j))

    lax.fori_loop(blocks - 1, blocks, within, 0)

    for j in range(1, GROUP):
        pl.when(z_in >= j)(functools.partial(z_take, j))
    logs, before = [], jnp.zeros((1, heads), F32)
    for k in range(GROUP - 1):
        log = jnp.where(k < z_in, zl[k][0:1, 0:heads], 0.0)
        logs.append(log)
        before = before + log
    decay_z = spread_rows(jnp.exp(stack_rows(logs + [before, running], 8)))
    zin[...] = jnp.zeros(zin.shape, F32)
    for k in range(GROUP - 1):

        @pl.when(k < z_in)
        def _(k=k):
            zin[...] = zin[...] * decay_z[k : k + 1] + zr[k].astype(F32)

    def gate_copy(j, to):
        return pltpu.make_async_remote_copy(ps, pr, p_s.at[j], p_r.at[0], device_id=at_z(to), device_id_type=MESH)

    @pl.when(z == gate_z)
    def _():
        ps[...] = (zin[...] * decay_z[GROUP : GROUP + 1] + state).astype(BF16)
        for j in range(z_n - GROUP):
            gate_copy(j, GROUP + j).start()

    @pl.when(z >= GROUP)
    def _():
        gate_copy(0, z).wait_recv()
        zin[...] = zin[...] + pr[...].astype(F32) * decay_z[GROUP - 1 : GROUP]

    for k in range(X):
        bs[k] = (pre[k] + zin[...] * decay_row[X + k : X + k + 1]).astype(BF16)

    def back_copy(j):
        k = x_peer(j)
        return pltpu.make_async_remote_copy(
            bs.at[k], br.at[x_at], back_s.at[j], back_r.at[j], device_id=at_x(k), device_id_type=MESH
        )

    for j in (2, 1, 3):
        back_copy(j).start()
    br[x_at] = bs[x_at]
    loads[5].wait()
    for j in range(1, X):
        back_copy(j).wait_recv()
    for k in range(X):
        came = br[k]
        passed = (came.astype(F32) * decay_core[0:1] + cbuf[0, k].astype(F32)).astype(BF16)
        cs[k] = jnp.where(core == 0, passed, came)
        ubuf[core, k] = jnp.where(core == 0, came, passed)
    core_back = pltpu.make_async_remote_copy(
        cs, ubuf.at[core], core_s.at[2], core_r.at[2], device_id=sibling, device_id_type=MESH
    )
    core_back.start()
    core_back.wait_recv()

    def norm(d):
        rows = pl.ds(pl.multiple_of(d * BLOCK, BLOCK), BLOCK)
        led = lead[d]
        squares = jnp.zeros((BLOCK, 1), F32)
        c_rows = c_b[rows, :]
        cols = cols_b[d]
        for t in range(width // tile):
            lanes = slice(t * tile, (t + 1) * tile)
            came = ubuf[:, :, :, lanes].reshape(N, tile).astype(F32)
            entering = (sent[d, :, lanes] + led[0:1, lanes] * came).astype(BF16)
            ssd = yw[rows, lanes] + dot(c_rows, entering) * dot(cols, spread_col[2, :, lanes])
            gated = ssd * sg[rows, lanes]
            squares = squares + jnp.sum(gated * gated, axis=1, keepdims=True)
            sg[rows, lanes] = gated
        scale = lax.rsqrt(squares * (1.0 / width) + 1e-05)
        for t in range(width // tile):
            lanes = slice(t * tile, (t + 1) * tile)
            nb[rows, lanes] = (sg[rows, lanes] * scale * ng_ref[:, lanes]).astype(BF16)

    def product(d, p):
        rows = pl.ds(pl.multiple_of(d * BLOCK, BLOCK), BLOCK)
        return dot(nb[rows, :], wv[:, pl.ds(pl.multiple_of(p * PIECE, PIECE), PIECE)])

    def far_right(i):
        return pltpu.make_async_remote_copy(
            so.at[i], ro_left.at[i], sum_s.at[i], sum_r.at[i], device_id=(me, right), device_id_type=MESH
        )

    def far_left(i):
        return pltpu.make_async_remote_copy(
            so.at[half + i], ro_right.at[i], sum_s.at[half + i], sum_r.at[half + i],
            device_id=(me, left), device_id_type=MESH,
        )

    def to_right(p):
        return pltpu.make_async_remote_copy(
            s_right.at[p], rf_left.at[p], sum_s.at[pieces + p], sum_r.at[pieces + p],
            device_id=(me, right), device_id_type=MESH,
        )

    def to_left(p):
        return pltpu.make_async_remote_copy(
            s_left.at[p], rf_right.at[p], sum_s.at[2 * pieces + p], sum_r.at[2 * pieces + p],
            device_id=(me, left), device_id_type=MESH,
        )

    norm(opp)

    def far_step(i, carry):
        so[i] = product(opp, i).astype(BF16)
        far_right(i).start()
        so[half + i] = product(opp, half + i).astype(BF16)
        far_left(i).start()
        return carry

    lax.fori_loop(0, half, far_step, 0)
    norm(right)
    norm(left)

    def near_step(i, carry):
        s_right[half + i] = product(right, half + i).astype(BF16)
        to_right(half + i).start()
        s_left[i] = product(left, i).astype(BF16)
        to_left(i).start()
        return carry

    lax.fori_loop(0, half, near_step, 0)
    norm(y)

    def own_step(p, carry):
        own[p] = product(y, p)
        return carry

    lax.fori_loop(0, pieces, own_step, 0)

    def sum_step(i, carry):
        ahead_right = product(right, i)
        ahead_left = product(left, half + i)
        far_right(i).wait_recv()
        s_right[i] = (ahead_right + ro_left[i].astype(F32)).astype(BF16)
        to_right(i).start()
        far_left(i).wait_recv()
        s_left[half + i] = (ahead_left + ro_right[i].astype(F32)).astype(BF16)
        to_left(half + i).start()
        return carry

    lax.fori_loop(0, half, sum_step, 0)

    def last_step(i, carry):
        for p in (i, half + i):
            to_right(p).wait_recv()
            to_left(p).wait_recv()
            ob[:, pl.ds(pl.multiple_of(p * PIECE, PIECE), PIECE)] = (
                own[p] + rf_left[p].astype(F32) + rf_right[p].astype(F32)
            ).astype(BF16)
        return carry

    lax.fori_loop(0, half, last_step, 0)

    for copy in (core_log, core_state, core_back):
        copy.wait_send()
    for j in range(1, X):
        for copy in x_copies(j):
            copy.wait_send()
        back_copy(j).wait_send()
    for j in range(1, GROUP):
        pl.when(z_in + j < GROUP)(functools.partial(z_sent, j))

    @pl.when(z == gate_z)
    def _():
        for j in range(z_n - GROUP):
            gate_copy(j, GROUP + j).wait_send()

    def drain(i, carry):
        far_right(i).wait_send()
        far_left(i).wait_send()
        for p in (i, half + i):
            to_right(p).wait_send()
            to_left(p).wait_send()
        return carry

    lax.fori_loop(0, half, drain, 0)


def solution(mesh):
    y_n = mesh.shape["head"]
    z_n = mesh.shape["seq"] // ROW

    def per_device(x, g, sr, dl, b, c, sk, ng, w):
        tokens, width = x.shape
        heads = dl.shape[0]
        dout = w.shape[1]
        blocks = tokens // BLOCK
        pieces = dout // PIECE
        slab = N // ROW
        hbm_spec = pl.BlockSpec(memory_space=pltpu.HBM)
        vmem_spec = pl.BlockSpec(memory_space=pltpu.VMEM)
        dma = pltpu.SemaphoreType.DMA
        vmem = pltpu.VMEM
        half = (pieces // 2, BLOCK, PIECE)
        full = (pieces, BLOCK, PIECE)
        rows = (X, slab, width)
        log = (8, LANES)
        return pl.pallas_call(
            functools.partial(kernel, z_n, y_n),
            out_shape=jax.ShapeDtypeStruct((tokens // y_n, dout), BF16),
            in_specs=[hbm_spec] * 3 + [vmem_spec] + [hbm_spec] * 2 + [vmem_spec] * 2 + [hbm_spec],
            out_specs=vmem_spec,
            scratch_shapes=[
                vmem((tokens, width), F32), vmem((tokens, width), BF16), vmem((heads, tokens), F32),
                vmem((tokens, N), F32), vmem((tokens, N), F32), vmem(w.shape, BF16),
                vmem((heads, width), BF16), vmem((4, 4 * heads, width), BF16), vmem((blocks, heads, BLOCK), F32),
                vmem((blocks, BLOCK, 4 * heads), F32), vmem((blocks, BLOCK, 4 * heads), BF16),
                vmem((blocks, N, BLOCK), BF16), vmem((tokens, N), BF16),
                vmem((blocks, N, width), F32), vmem((blocks, 8, width), F32),
                vmem((CORES,) + rows, BF16), vmem((CORES,) + rows, BF16),
                vmem(rows, BF16), vmem(rows, BF16), vmem(rows, BF16), vmem(rows, BF16), vmem(rows, BF16),
                vmem((CORES,) + rows, BF16),
                vmem((slab, width), BF16), vmem((GROUP, slab, width), BF16),
                vmem((slab, width), BF16), vmem((slab, width), BF16),
                vmem(log, F32), vmem((CORES,) + log, F32), vmem(log, F32), vmem((X,) + log, F32),
                vmem(log, F32), vmem((GROUP,) + log, F32), vmem(rows, F32), vmem((slab, width), F32),
                vmem((tokens, width), F32), vmem((tokens, width), F32), vmem((tokens, width), BF16),
                vmem(full, F32),
                vmem(full, BF16), vmem(full, BF16), vmem(full, BF16),
                vmem(half, BF16), vmem(half, BF16), vmem(full, BF16), vmem(full, BF16),
                dma((6,)), dma((3,)), dma((3,)), dma((X,)), dma((X,)), dma((X,)), dma((X,)),
                dma((GROUP,)), dma((GROUP,)), dma((GROUP,)), dma((GROUP,)),
                dma((z_n - GROUP,)), dma((1,)), dma((X,)), dma((X,)),
                dma((3 * pieces,)), dma((3 * pieces,)),
            ],
            compiler_params=pltpu.CompilerParams(
                collective_id=0, has_side_effects=True, vmem_limit_bytes=58 * 1024 * 1024
            ),
        )(
            x, g, sr.T, dl.reshape(1, heads), b.reshape(tokens, N), c.reshape(tokens, N),
            sk.reshape(1, heads), ng.reshape(1, width), w,
        )

    in_specs = (
        P("seq", "head"), P("seq", "head"), P("seq", "head"), P("head"), P("seq", "head", None),
        P("seq", "head", None), P("head"), P("head"), P("head", None),
    )
    return jax.shard_map(
        per_device, mesh=mesh, in_specs=in_specs, out_specs=P(("seq", "head"), None), check_vma=False
    )
```

time: 73 us -> 65.1 us (0.89)
  the two profiles are of different devices: /device:TPU:1 before, /device:TPU:225 now
where the time goes in v2:
time: 65.1 us; the launch traced here: 64.5 us
  Pallas kernels  62.2 us (96%)
  local copies, waits for them, and re-layouts  2.29 us (4%)
    pallas_call x1, Pallas kernels, per_device(): pl.pallas_call(functools.partial(kernel, z_n, y_n), out_shape=jax.ShapeDt...  62.2 us
    unnamed x1, local copies, waits for them, and re-layouts  2.29 us

profile of v2, /device:TPU:225, one launch (start us, length us, event | category | flops | bytes accessed | tf_op | source)
XLA Modules:
  0.0 64.5 jit_solution(12329237856453731480)
XLA Ops:
  0.0 62.2 %shard_map.91 = bf16[128,4096]{1,0:T(8,128)(2,1)} custom-call(f32[512,1024]{1,0:T(8,128)} %x_hbm.1, bf16[512,1024]{1,0:T(8,128)(2,1)} %g_hbm.1, f32[16,512]{1,0:T(8,128)} %bitcast.8, f32[1,16]{1,0:T(1,128)} %bitcast.10, f32[512,128]{1,0:T(8,128)} %bitcast.6, f32[512,128]{1,0:T(8,128)} %bitcast.7, f32[1,16]{1,0:T(1,128)} %bitcast.11, f32[1,1024]{1,0:T(1,128)} %bitcast.9, ...), custom_call_target="tpu_custom_call" | custom-call | tf_op jit(solution)/shard_map/pallas_call | solution.py:464
  62.2 2.3 %copy.11 = bf16[128,4096]{1,0:T(8,128)(2,1)} copy(bf16[128,4096]{1,0:T(8,128)(2,1)} %shard_map.91) | data formatting | bytes 2097152

commit v3 on v2

--- a/solution.py
+++ b/solution.py
@@ -15,7 +15,10 @@
 X = 4
 ROW = CORES * X
 GROUP = 4
-PIECE = 512
+CHUNKS = 3
+RING = 7
+FAR_A = 4
+PIECE = 256
 LANES = 128
 EXACT = lax.Precision.HIGHEST
 MESH = pl.DeviceIdType.MESH
@@ -45,22 +48,21 @@
     spread, spread_col, cum_t, cols_s, cols_b, b_t, c_b,
     sent, lead, sbuf, cbuf, xs, xr, bs, br, cs, ubuf, zs, zr, ps, pr,
     lt, cl, xt, xl, zt, zl, pre, zin,
-    yw, sg, nb, own,
-    so, s_right, s_left, ro_left, ro_right, rf_left, rf_right,
+    yw, sg, nl, na, nq, own_r, own_p,
+    so, s_a, s_b, ro, rf_a, rf_b, pb, rb, wp,
     in_sem, core_s, core_r, x_s, x_r, xlog_s, xlog_r, z_s, z_r, zlog_s, zlog_r, p_s, p_r, back_s, back_r, sum_s, sum_r,
+    n_s, n_r, pair_s, pair_r, wa_s, wa_r, wx_s, wx_r, ws_s, ws_r,
 ):
     tokens, width = xv.shape
     heads = srv.shape[0]
     blocks = tokens // BLOCK
-    pieces = wv.shape[1] // PIECE
-    half = pieces // 2
     slab = N // ROW
     me = lax.axis_index("seq")
     y = lax.axis_index("head")
     z, r = lax.div(me, ROW), lax.rem(me, ROW)
     x_at, core = lax.div(r, CORES), lax.rem(r, CORES)
     z_in = lax.rem(z, GROUP)
-    right, left, opp = lax.rem(y + 1, y_n), lax.rem(y + y_n - 1, y_n), lax.rem(y + 2, y_n)
+    a_at, b_at, opp = y + 1 - 2 * lax.rem(y, 2), y_n - 1 - y, lax.rem(y + 2, y_n)
     sibling = (me + 1 - 2 * core, y)
     gate_z = GROUP - 1
 
@@ -81,8 +83,8 @@
     greet(sibling)
     for j in range(1, X):
         greet(at_x(x_peer(j)))
-    greet((me, right))
-    greet((me, left))
+    greet((me, a_at))
+    greet((me, b_at))
     for j in range(1, GROUP):
         pl.when(z_in >= j)(functools.partial(greet, at_z(z - j)))
     pl.when(z >= GROUP)(functools.partial(greet, at_z(gate_z)))
@@ -141,6 +143,43 @@
     loads[2].wait()
     for load in loads[3:]:
         load.start()
+    pl.semaphore_wait(barrier, X + 2 + (GROUP - 1 - z_in) + jnp.where(z == gate_z, z_n - GROUP, 0))
+
+    up, down = x_peer(1), x_peer(X - 1)
+    near_piece = CORES * x_at + core
+
+    def column(piece, k):
+        quarter = lax.div(piece, CORES) * (wv.shape[1] // X)
+        return pl.multiple_of(quarter + lax.rem(piece, CORES) * CHUNKS * LANES + k * LANES, LANES)
+
+    def w_first(k):
+        return pltpu.make_async_remote_copy(
+            w_hbm.at[:, pl.ds(column(near_piece, k), LANES)], wp.at[near_piece, k], wa_s.at[k], wa_r.at[k],
+            device_id=(me, a_at), device_id_type=MESH,
+        )
+
+    def w_beside(side, k):
+        return pltpu.make_async_remote_copy(
+            wp.at[near_piece, k], wp.at[near_piece, k], wx_s.at[side * CHUNKS + k], wx_r.at[side * CHUNKS + k],
+            device_id=at_x(up if side == 0 else down), device_id_type=MESH,
+        )
+
+    def w_sibling(source, k):
+        piece = CORES * (x_at, down, up)[source] + core
+        return pltpu.make_async_remote_copy(
+            wp.at[piece, k], wp.at[piece, k], ws_s.at[source * CHUNKS + k], ws_r.at[source * CHUNKS + k],
+            device_id=sibling, device_id_type=MESH,
+        )
+
+    def w_pass(k):
+        w_first(k).wait_recv()
+        w_beside(0, k).start()
+        w_beside(1, k).start()
+        w_sibling(0, k).start()
+
+    for k in range(CHUNKS):
+        w_first(k).start()
+
     tile = 256
     for t in range(width // tile):
         lanes = slice(t * tile, (t + 1) * tile)
@@ -151,8 +190,6 @@
             ended = (xv[rows, lanes] * dot(cols_b[c], spread_col[1, :, lanes])).astype(BF16)
             state = state * factors[c : c + 1, lanes] + dot(b_t[c], ended)
         sbuf[:, :, :, lanes] = state.astype(BF16).reshape(CORES, X, slab, tile)
-
-    pl.semaphore_wait(barrier, X + 2 + (GROUP - 1 - z_in) + jnp.where(z == gate_z, z_n - GROUP, 0))
 
     core_log = pltpu.make_async_remote_copy(
         lt, cl.at[core], core_s.at[0], core_r.at[0], device_id=sibling, device_id_type=MESH
@@ -261,36 +298,44 @@
     for j in range(1, GROUP):
         pl.when(z_in + j < GROUP)(functools.partial(z_send, j))
 
-    lax.fori_loop(blocks - 1, blocks, within, 0)
-
-    for j in range(1, GROUP):
-        pl.when(z_in >= j)(functools.partial(z_take, j))
-    logs, before = [], jnp.zeros((1, heads), F32)
-    for k in range(GROUP - 1):
-        log = jnp.where(k < z_in, zl[k][0:1, 0:heads], 0.0)
-        logs.append(log)
-        before = before + log
-    decay_z = spread_rows(jnp.exp(stack_rows(logs + [before, running], 8)))
-    zin[...] = jnp.zeros(zin.shape, F32)
-    for k in range(GROUP - 1):
-
-        @pl.when(k < z_in)
-        def _(k=k):
-            zin[...] = zin[...] * decay_z[k : k + 1] + zr[k].astype(F32)
+    def join_z():
+        for j in range(1, GROUP):
+            pl.when(z_in >= j)(functools.partial(z_take, j))
+        logs, before = [], jnp.zeros((1, heads), F32)
+        for k in range(GROUP - 1):
+            log = jnp.where(k < z_in, zl[k][0:1, 0:heads], 0.0)
+            logs.append(log)
+            before = before + log
+        decay_z = spread_rows(jnp.exp(stack_rows(logs + [before, running], 8)))
+        zin[...] = jnp.zeros(zin.shape, F32)
+        for k in range(GROUP - 1):
+
+            @pl.when(k < z_in)
+            def _(k=k):
+                zin[...] = zin[...] * decay_z[k : k + 1] + zr[k].astype(F32)
+
+        return decay_z
 
     def gate_copy(j, to):
         return pltpu.make_async_remote_copy(ps, pr, p_s.at[j], p_r.at[0], device_id=at_z(to), device_id_type=MESH)
 
     @pl.when(z == gate_z)
     def _():
+        decay_z = join_z()
         ps[...] = (zin[...] * decay_z[GROUP : GROUP + 1] + state).astype(BF16)
-        for j in range(z_n - GROUP):
+        for j in range(z_n - GROUP - 1, -1, -1):
             gate_copy(j, GROUP + j).start()
 
-    @pl.when(z >= GROUP)
+    lax.fori_loop(blocks - 1, blocks, within, 0)
+
+    @pl.when(z != gate_z)
     def _():
-        gate_copy(0, z).wait_recv()
-        zin[...] = zin[...] + pr[...].astype(F32) * decay_z[GROUP - 1 : GROUP]
+        decay_z = join_z()
+
+        @pl.when(z >= GROUP)
+        def _():
+            gate_copy(0, z).wait_recv()
+            zin[...] = zin[...] + pr[...].astype(F32) * decay_z[GROUP - 1 : GROUP]
 
     for k in range(X):
         bs[k] = (pre[k] + zin[...] * decay_row[X + k : X + k + 1]).astype(BF16)
@@ -299,26 +344,31 @@
         k = x_peer(j)
         return pltpu.make_async_remote_copy(
             bs.at[k], br.at[x_at], back_s.at[j], back_r.at[j], device_id=at_x(k), device_id_type=MESH
+        )
+
+    def core_back(j):
+        k = lax.rem(x_at + X - j, X)
+        return pltpu.make_async_remote_copy(
+            cs.at[k], ubuf.at[core, k], core_s.at[2 + j], core_r.at[2 + j], device_id=sibling, device_id_type=MESH
         )
 
     for j in (2, 1, 3):
         back_copy(j).start()
     br[x_at] = bs[x_at]
     loads[5].wait()
-    for j in range(1, X):
-        back_copy(j).wait_recv()
-    for k in range(X):
+    for j in (0, 1, 3, 2):
+        if j:
+            back_copy(j).wait_recv()
+        k = lax.rem(x_at + X - j, X)
         came = br[k]
         passed = (came.astype(F32) * decay_core[0:1] + cbuf[0, k].astype(F32)).astype(BF16)
         cs[k] = jnp.where(core == 0, passed, came)
         ubuf[core, k] = jnp.where(core == 0, came, passed)
-    core_back = pltpu.make_async_remote_copy(
-        cs, ubuf.at[core], core_s.at[2], core_r.at[2], device_id=sibling, device_id_type=MESH
-    )
-    core_back.start()
-    core_back.wait_recv()
-
-    def norm(d):
+        core_back(j).start()
+    for j in range(X):
+        core_back(j).wait_recv()
+
+    def norm(d, into, at):
         rows = pl.ds(pl.multiple_of(d * BLOCK, BLOCK), BLOCK)
         led = lead[d]
         squares = jnp.zeros((BLOCK, 1), F32)
@@ -335,90 +385,157 @@
         scale = lax.rsqrt(squares * (1.0 / width) + 1e-05)
         for t in range(width // tile):
             lanes = slice(t * tile, (t + 1) * tile)
-            nb[rows, lanes] = (sg[rows, lanes] * scale * ng_ref[:, lanes]).astype(BF16)
-
-    def product(d, p):
-        rows = pl.ds(pl.multiple_of(d * BLOCK, BLOCK), BLOCK)
-        return dot(nb[rows, :], wv[:, pl.ds(pl.multiple_of(p * PIECE, PIECE), PIECE)])
-
-    def far_right(i):
-        return pltpu.make_async_remote_copy(
-            so.at[i], ro_left.at[i], sum_s.at[i], sum_r.at[i], device_id=(me, right), device_id_type=MESH
-        )
-
-    def far_left(i):
-        return pltpu.make_async_remote_copy(
-            so.at[half + i], ro_right.at[i], sum_s.at[half + i], sum_r.at[half + i],
-            device_id=(me, left), device_id_type=MESH,
-        )
-
-    def to_right(p):
-        return pltpu.make_async_remote_copy(
-            s_right.at[p], rf_left.at[p], sum_s.at[pieces + p], sum_r.at[pieces + p],
-            device_id=(me, right), device_id_type=MESH,
-        )
-
-    def to_left(p):
-        return pltpu.make_async_remote_copy(
-            s_left.at[p], rf_right.at[p], sum_s.at[2 * pieces + p], sum_r.at[2 * pieces + p],
-            device_id=(me, left), device_id_type=MESH,
-        )
-
-    norm(opp)
-
-    def far_step(i, carry):
-        so[i] = product(opp, i).astype(BF16)
-        far_right(i).start()
-        so[half + i] = product(opp, half + i).astype(BF16)
-        far_left(i).start()
+            into[at : at + BLOCK, lanes] = (sg[rows, lanes] * scale * ng_ref[:, lanes]).astype(BF16)
+
+    def ring_columns(i):
+        quarter = wv.shape[1] // X
+        if i < X:
+            start = x_peer(2) * quarter + i * PIECE
+        else:
+            start = x_peer((0, 1, X - 1)[i - X]) * quarter + CORES * CHUNKS * LANES
+        return pl.ds(pl.multiple_of(start, PIECE), PIECE)
+
+    def product(of, at, i):
+        return dot(of[at : at + BLOCK, :], wv[:, ring_columns(i)])
+
+    def far(i):
+        return pltpu.make_async_remote_copy(
+            so.at[i], ro.at[i], sum_s.at[i], sum_r.at[i],
+            device_id=(me, a_at if i < FAR_A else b_at), device_id_type=MESH,
+        )
+
+    def to_a(i):
+        return pltpu.make_async_remote_copy(
+            s_a.at[i], rf_a.at[i], sum_s.at[RING + i], sum_r.at[RING + i], device_id=(me, a_at), device_id_type=MESH
+        )
+
+    def to_b(i):
+        return pltpu.make_async_remote_copy(
+            s_b.at[i], rf_b.at[i], sum_s.at[2 * RING + i], sum_r.at[2 * RING + i],
+            device_id=(me, b_at), device_id_type=MESH,
+        )
+
+    def n_copy(i):
+        rows = slice(i * BLOCK, (i + 1) * BLOCK)
+        return pltpu.make_async_remote_copy(
+            na.at[rows, :], nq.at[rows, :], n_s.at[i], n_r.at[i], device_id=(me, a_at), device_id_type=MESH
+        )
+
+    def pair_copy(piece, k):
+        where = piece * CHUNKS + k
+        return pltpu.make_async_remote_copy(
+            pb.at[piece, k], rb.at[piece, k], pair_s.at[where], pair_r.at[where],
+            device_id=(me, b_at), device_id_type=MESH,
+        )
+
+    def pair(rows, piece, k):
+        columns = pl.ds(column(piece, k), LANES)
+        return dot(nl[rows, :], wv[:, columns]) + dot(nq[rows, :], wp[piece, k])
+
+    b_rows, own_rows, both_rows = slice(0, BLOCK), slice(BLOCK, 2 * BLOCK), slice(0, 2 * BLOCK)
+
+    def pair_b(piece, k):
+        pb[piece, k] = pair(b_rows, piece, k).astype(BF16)
+        pair_copy(piece, k).start()
+
+    def pair_own(piece, k):
+        own_p[piece, k] = pair(own_rows, piece, k)
+
+    def pair_both(piece, k):
+        total = pair(both_rows, piece, k)
+        pb[piece, k] = total[b_rows].astype(BF16)
+        pair_copy(piece, k).start()
+        own_p[piece, k] = total[own_rows]
+
+    norm(opp, na, 0)
+    n_copy(0).start()
+    for i in (4, 0, 5, 1, 6, 2, 3):
+        so[i] = product(na, 0, i).astype(BF16)
+        far(i).start()
+    norm(a_at, na, BLOCK)
+    n_copy(1).start()
+    w_pass(0)
+    w_pass(1)
+    norm(b_at, nl, 0)
+    for i in range(FAR_A, RING):
+        s_b[i] = product(nl, 0, i).astype(BF16)
+        to_b(i).start()
+    for i in range(FAR_A):
+        s_a[i] = product(na, BLOCK, i).astype(BF16)
+        to_a(i).start()
+    w_pass(2)
+    norm(y, nl, BLOCK)
+    for i in range(RING):
+        own_r[i] = product(nl, BLOCK, i)
+    n_copy(0).wait_recv()
+    beside_piece = CORES * x_at + 1 - core
+
+    def near_b(k, carry):
+        pair_b(near_piece, k)
+        w_sibling(0, k).wait_recv()
+        pair_b(beside_piece, k)
         return carry
 
-    lax.fori_loop(0, half, far_step, 0)
-    norm(right)
-    norm(left)
-
-    def near_step(i, carry):
-        s_right[half + i] = product(right, half + i).astype(BF16)
-        to_right(half + i).start()
-        s_left[i] = product(left, i).astype(BF16)
-        to_left(i).start()
+    lax.fori_loop(0, CHUNKS, near_b, 0)
+    for i in range(FAR_A):
+        ahead = product(nl, 0, i)
+        far(i).wait_recv()
+        s_b[i] = (ahead + ro[i].astype(F32)).astype(BF16)
+        to_b(i).start()
+    for i in range(FAR_A, RING):
+        ahead = product(na, BLOCK, i)
+        far(i).wait_recv()
+        s_a[i] = (ahead + ro[i].astype(F32)).astype(BF16)
+        to_a(i).start()
+    n_copy(1).wait_recv()
+
+    def near_own(k, carry):
+        pair_own(near_piece, k)
+        pair_own(beside_piece, k)
         return carry
 
-    lax.fori_loop(0, half, near_step, 0)
-    norm(y)
-
-    def own_step(p, carry):
-        own[p] = product(y, p)
+    lax.fori_loop(0, CHUNKS, near_own, 0)
+
+    def side_both(k, carry):
+        for side, at in ((0, down), (1, up)):
+            w_beside(side, k).wait_recv()
+            w_sibling(1 + side, k).start()
+        for at in (down, up):
+            pair_both(CORES * at + core, k)
+        for side, at in ((0, down), (1, up)):
+            w_sibling(1 + side, k).wait_recv()
+            pair_both(CORES * at + 1 - core, k)
         return carry
 
-    lax.fori_loop(0, pieces, own_step, 0)
-
-    def sum_step(i, carry):
-        ahead_right = product(right, i)
-        ahead_left = product(left, half + i)
-        far_right(i).wait_recv()
-        s_right[i] = (ahead_right + ro_left[i].astype(F32)).astype(BF16)
-        to_right(i).start()
-        far_left(i).wait_recv()
-        s_left[half + i] = (ahead_left + ro_right[i].astype(F32)).astype(BF16)
-        to_left(half + i).start()
+    lax.fori_loop(0, CHUNKS, side_both, 0)
+
+    def finish(piece, k):
+        pair_copy(piece, k).wait_recv()
+        ob[:, pl.ds(column(piece, k), LANES)] = (own_p[piece, k] + rb[piece, k].astype(F32)).astype(BF16)
+
+    def near_last(k, carry):
+        finish(near_piece, k)
+        finish(beside_piece, k)
         return carry
 
-    lax.fori_loop(0, half, sum_step, 0)
-
-    def last_step(i, carry):
-        for p in (i, half + i):
-            to_right(p).wait_recv()
-            to_left(p).wait_recv()
-            ob[:, pl.ds(pl.multiple_of(p * PIECE, PIECE), PIECE)] = (
-                own[p] + rf_left[p].astype(F32) + rf_right[p].astype(F32)
-            ).astype(BF16)
+    lax.fori_loop(0, CHUNKS, near_last, 0)
+    for i in range(RING):
+        to_a(i).wait_recv()
+        to_b(i).wait_recv()
+        ob[:, ring_columns(i)] = (own_r[i] + rf_a[i].astype(F32) + rf_b[i].astype(F32)).astype(BF16)
+
+    def side_last(k, carry):
+        for c in range(CORES):
+            for at in (down, up):
+                finish(CORES * at + lax.rem(core + c, CORES), k)
         return carry
 
-    lax.fori_loop(0, half, last_step, 0)
-
-    for copy in (core_log, core_state, core_back):
-        copy.wait_send()
+    lax.fori_loop(0, CHUNKS, side_last, 0)
+
+    core_log.wait_send()
+    core_state.wait_send()
+    for j in range(X):
+        core_back(j).wait_send()
     for j in range(1, X):
         for copy in x_copies(j):
             copy.wait_send()
@@ -431,15 +548,24 @@
         for j in range(z_n - GROUP):
             gate_copy(j, GROUP + j).wait_send()
 
-    def drain(i, carry):
-        far_right(i).wait_send()
-        far_left(i).wait_send()
-        for p in (i, half + i):
-            to_right(p).wait_send()
-            to_left(p).wait_send()
+    for i in range(RING):
+        far(i).wait_send()
+        to_a(i).wait_send()
+        to_b(i).wait_send()
+    n_copy(0).wait_send()
+    n_copy(1).wait_send()
+
+    def drain(k, carry):
+        w_first(k).wait_send()
+        for side in range(2):
+            w_beside(side, k).wait_send()
+        for source, at in enumerate((x_at, down, up)):
+            w_sibling(source, k).wait_send()
+            for c in range(CORES):
+                pair_copy(CORES * at + c, k).wait_send()
         return carry
 
-    lax.fori_loop(0, half, drain, 0)
+    lax.fori_loop(0, CHUNKS, drain, 0)
 
 
 def solution(mesh):
@@ -451,14 +577,15 @@
         heads = dl.shape[0]
         dout = w.shape[1]
         blocks = tokens // BLOCK
-        pieces = dout // PIECE
+        pieces = X * CORES
         slab = N // ROW
         hbm_spec = pl.BlockSpec(memory_space=pltpu.HBM)
         vmem_spec = pl.BlockSpec(memory_space=pltpu.VMEM)
         dma = pltpu.SemaphoreType.DMA
         vmem = pltpu.VMEM
-        half = (pieces // 2, BLOCK, PIECE)
-        full = (pieces, BLOCK, PIECE)
+        ring = (RING, BLOCK, PIECE)
+        chunks = (pieces, CHUNKS, BLOCK, LANES)
+        normed = (2 * BLOCK, width)
         rows = (X, slab, width)
         log = (8, LANES)
         return pl.pallas_call(
@@ -480,14 +607,16 @@
                 vmem((slab, width), BF16), vmem((slab, width), BF16),
                 vmem(log, F32), vmem((CORES,) + log, F32), vmem(log, F32), vmem((X,) + log, F32),
                 vmem(log, F32), vmem((GROUP,) + log, F32), vmem(rows, F32), vmem((slab, width), F32),
-                vmem((tokens, width), F32), vmem((tokens, width), F32), vmem((tokens, width), BF16),
-                vmem(full, F32),
-                vmem(full, BF16), vmem(full, BF16), vmem(full, BF16),
-                vmem(half, BF16), vmem(half, BF16), vmem(full, BF16), vmem(full, BF16),
-                dma((6,)), dma((3,)), dma((3,)), dma((X,)), dma((X,)), dma((X,)), dma((X,)),
+                vmem((tokens, width), F32), vmem((tokens, width), F32),
+                vmem(normed, BF16), vmem(normed, BF16), vmem(normed, BF16), vmem(ring, F32), vmem(chunks, F32),
+                vmem(ring, BF16), vmem(ring, BF16), vmem(ring, BF16), vmem(ring, BF16), vmem(ring, BF16), vmem(ring, BF16),
+                vmem(chunks, BF16), vmem(chunks, BF16), vmem((pieces, CHUNKS, width, LANES), BF16),
+                dma((6,)), dma((2 + X,)), dma((2 + X,)), dma((X,)), dma((X,)), dma((X,)), dma((X,)),
                 dma((GROUP,)), dma((GROUP,)), dma((GROUP,)), dma((GROUP,)),
                 dma((z_n - GROUP,)), dma((1,)), dma((X,)), dma((X,)),
-                dma((3 * pieces,)), dma((3 * pieces,)),
+                dma((3 * RING,)), dma((3 * RING,)), dma((2,)), dma((2,)), dma((pieces * CHUNKS,)), dma((pieces * CHUNKS,)),
+                dma((CHUNKS,)), dma((CHUNKS,)), dma((2 * CHUNKS,)), dma((2 * CHUNKS,)),
+                dma((3 * CHUNKS,)), dma((3 * CHUNKS,)),
             ],
             compiler_params=pltpu.CompilerParams(
                 collective_id=0, has_side_effects=True, vmem_limit_bytes=58 * 1024 * 1024

time: 65.1 us -> 62.2 us (0.955)
  Pallas kernels: 62.2 us -> 58.8 us
    pallas_call x1, Pallas kernels: 62.2 us -> 58.8 us  [per_device(): pl.pallas_call(functools.partial(kernel, z_n, y_n), out_shape=jax.ShapeDt...]
where the time goes in v3:
time: 62.2 us; the launch traced here: 61.1 us
  Pallas kernels  58.8 us (95%)
  local copies, waits for them, and re-layouts  2.29 us (4%)
    pallas_call x1, Pallas kernels, per_device(): pl.pallas_call(functools.partial(kernel, z_n, y_n), out_shape=jax.ShapeDt...  58.8 us
    unnamed x1, local copies, waits for them, and re-layouts  2.29 us

profile of v3, /device:TPU:225, one launch (start us, length us, event | category | flops | bytes accessed | tf_op | source)
XLA Modules:
  0.0 61.1 jit_solution(9278874868992419182)
XLA Ops:
  0.0 58.8 %shard_map.91 = bf16[128,4096]{1,0:T(8,128)(2,1)} custom-call(f32[512,1024]{1,0:T(8,128)} %x_hbm.1, bf16[512,1024]{1,0:T(8,128)(2,1)} %g_hbm.1, f32[16,512]{1,0:T(8,128)} %bitcast.8, f32[1,16]{1,0:T(1,128)} %bitcast.10, f32[512,128]{1,0:T(8,128)} %bitcast.6, f32[512,128]{1,0:T(8,128)} %bitcast.7, f32[1,16]{1,0:T(1,128)} %bitcast.11, f32[1,1024]{1,0:T(1,128)} %bitcast.9, ...), custom_call_target="tpu_custom_call" | custom-call | tf_op jit(solution)/shard_map/pallas_call | solution.py:591
  58.8 2.3 %copy.11 = bf16[128,4096]{1,0:T(8,128)(2,1)} copy(bf16[128,4096]{1,0:T(8,128)(2,1)} %shard_map.91) | data formatting | bytes 2097152

commit v4 on v3

--- a/solution.py
+++ b/solution.py
@@ -432,7 +432,7 @@
         columns = pl.ds(column(piece, k), LANES)
         return dot(nl[rows, :], wv[:, columns]) + dot(nq[rows, :], wp[piece, k])
 
-    b_rows, own_rows, both_rows = slice(0, BLOCK), slice(BLOCK, 2 * BLOCK), slice(0, 2 * BLOCK)
+    b_rows, own_rows = slice(0, BLOCK), slice(BLOCK, 2 * BLOCK)
 
     def pair_b(piece, k):
         pb[piece, k] = pair(b_rows, piece, k).astype(BF16)
@@ -440,12 +440,6 @@
 
     def pair_own(piece, k):
         own_p[piece, k] = pair(own_rows, piece, k)
-
-    def pair_both(piece, k):
-        total = pair(both_rows, piece, k)
-        pb[piece, k] = total[b_rows].astype(BF16)
-        pair_copy(piece, k).start()
-        own_p[piece, k] = total[own_rows]
 
     norm(opp, na, 0)
     n_copy(0).start()
@@ -487,27 +481,34 @@
         far(i).wait_recv()
         s_a[i] = (ahead + ro[i].astype(F32)).astype(BF16)
         to_a(i).start()
-    n_copy(1).wait_recv()
 
     def near_own(k, carry):
         pair_own(near_piece, k)
         pair_own(beside_piece, k)
         return carry
 
-    lax.fori_loop(0, CHUNKS, near_own, 0)
-
-    def side_both(k, carry):
-        for side, at in ((0, down), (1, up)):
+    def side_b(k, carry):
+        for side in range(2):
             w_beside(side, k).wait_recv()
             w_sibling(1 + side, k).start()
         for at in (down, up):
-            pair_both(CORES * at + core, k)
+            pair_b(CORES * at + core, k)
         for side, at in ((0, down), (1, up)):
             w_sibling(1 + side, k).wait_recv()
-            pair_both(CORES * at + 1 - core, k)
-        return carry
-
-    lax.fori_loop(0, CHUNKS, side_both, 0)
+            pair_b(CORES * at + 1 - core, k)
+        return carry
+
+    def side_own(k, carry):
+        for at in (down, up):
+            for c in range(CORES):
+                pair_own(CORES * at + c, k)
+        return carry
+
+    lax.fori_loop(0, CHUNKS - 1, side_b, 0)
+    n_copy(1).wait_recv()
+    lax.fori_loop(0, CHUNKS, near_own, 0)
+    lax.fori_loop(CHUNKS - 1, CHUNKS, side_b, 0)
+    lax.fori_loop(0, CHUNKS, side_own, 0)
 
     def finish(piece, k):
         pair_copy(piece, k).wait_recv()

time: 62.2 us -> 59.5 us (0.957); the launches traced: 61.1 us -> 59.3 us
  Pallas kernels: 58.8 us -> 57 us
    pallas_call x1, Pallas kernels: 58.8 us -> 57 us  [per_device(): pl.pallas_call(functools.partial(kernel, z_n, y_n), out_shape=jax.ShapeDt...]
where the time goes in v4:
time: 59.5 us; the launch traced here: 59.3 us
  Pallas kernels  57 us (96%)
  local copies, waits for them, and re-layouts  2.29 us (4%)
    pallas_call x1, Pallas kernels, per_device(): pl.pallas_call(functools.partial(kernel, z_n, y_n), out_shape=jax.ShapeDt...  57 us
    unnamed x1, local copies, waits for them, and re-layouts  2.29 us

profile of v4, /device:TPU:225, one launch (start us, length us, event | category | flops | bytes accessed | tf_op | source)
XLA Modules:
  0.0 59.3 jit_solution(4627487501810961971)
XLA Ops:
  0.0 57.0 %shard_map.91 = bf16[128,4096]{1,0:T(8,128)(2,1)} custom-call(f32[512,1024]{1,0:T(8,128)} %x_hbm.1, bf16[512,1024]{1,0:T(8,128)(2,1)} %g_hbm.1, f32[16,512]{1,0:T(8,128)} %bitcast.8, f32[1,16]{1,0:T(1,128)} %bitcast.10, f32[512,128]{1,0:T(8,128)} %bitcast.6, f32[512,128]{1,0:T(8,128)} %bitcast.7, f32[1,16]{1,0:T(1,128)} %bitcast.11, f32[1,1024]{1,0:T(1,128)} %bitcast.9, ...), custom_call_target="tpu_custom_call" | custom-call | tf_op jit(solution)/shard_map/pallas_call | solution.py:592
  57.0 2.3 %copy.11 = bf16[128,4096]{1,0:T(8,128)(2,1)} copy(bf16[128,4096]{1,0:T(8,128)(2,1)} %shard_map.91) | data formatting | bytes 2097152

commit v5 on v4

--- a/solution.py
+++ b/solution.py
@@ -143,8 +143,6 @@
     loads[2].wait()
     for load in loads[3:]:
         load.start()
-    pl.semaphore_wait(barrier, X + 2 + (GROUP - 1 - z_in) + jnp.where(z == gate_z, z_n - GROUP, 0))
-
     up, down = x_peer(1), x_peer(X - 1)
     near_piece = CORES * x_at + core
 
@@ -176,9 +174,6 @@
         w_beside(0, k).start()
         w_beside(1, k).start()
         w_sibling(0, k).start()
-
-    for k in range(CHUNKS):
-        w_first(k).start()
 
     tile = 256
     for t in range(width // tile):
@@ -191,6 +186,8 @@
             state = state * factors[c : c + 1, lanes] + dot(b_t[c], ended)
         sbuf[:, :, :, lanes] = state.astype(BF16).reshape(CORES, X, slab, tile)
 
+    pl.semaphore_wait(barrier, X + 2 + (GROUP - 1 - z_in) + jnp.where(z == gate_z, z_n - GROUP, 0))
+
     core_log = pltpu.make_async_remote_copy(
         lt, cl.at[core], core_s.at[0], core_r.at[0], device_id=sibling, device_id_type=MESH
     )
@@ -199,6 +196,8 @@
     )
     core_log.start()
     core_state.start()
+    for k in range(CHUNKS):
+        w_first(k).start()
     cl[core] = lt[...]
     cbuf[core] = sbuf[core]
     core_log.wait_recv()

time: 59.5 us -> 58.6 us (0.985)
  Pallas kernels: 57 us -> 56.2 us
    pallas_call x1, Pallas kernels: 57 us -> 56.2 us  [per_device(): pl.pallas_call(functools.partial(kernel, z_n, y_n), out_shape=jax.ShapeDt...]
where the time goes in v5:
time: 58.6 us; the launch traced here: 58.5 us
  Pallas kernels  56.2 us (96%)
  local copies, waits for them, and re-layouts  2.29 us (4%)
    pallas_call x1, Pallas kernels, per_device(): pl.pallas_call(functools.partial(kernel, z_n, y_n), out_shape=jax.ShapeDt...  56.2 us
    unnamed x1, local copies, waits for them, and re-layouts  2.29 us

profile of v5, /device:TPU:225, one launch (start us, length us, event | category | flops | bytes accessed | tf_op | source)
XLA Modules:
  0.0 58.5 jit_solution(9002354043079688968)
XLA Ops:
  0.0 56.2 %shard_map.91 = bf16[128,4096]{1,0:T(8,128)(2,1)} custom-call(f32[512,1024]{1,0:T(8,128)} %x_hbm.1, bf16[512,1024]{1,0:T(8,128)(2,1)} %g_hbm.1, f32[16,512]{1,0:T(8,128)} %bitcast.8, f32[1,16]{1,0:T(1,128)} %bitcast.10, f32[512,128]{1,0:T(8,128)} %bitcast.6, f32[512,128]{1,0:T(8,128)} %bitcast.7, f32[1,16]{1,0:T(1,128)} %bitcast.11, f32[1,1024]{1,0:T(1,128)} %bitcast.9, ...), custom_call_target="tpu_custom_call" | custom-call | tf_op jit(solution)/shard_map/pallas_call | solution.py:591
  56.2 2.3 %copy.11 = bf16[128,4096]{1,0:T(8,128)(2,1)} copy(bf16[128,4096]{1,0:T(8,128)(2,1)} %shard_map.91) | data formatting | bytes 2097152
